TPU v7x, 256 devices: a whole 4x4x8 slice. The times are simulated.
256 devices in a mesh: seq: 32 (over z, x), head: 8 (over y, core).
Axes of the slice: x: 4, y: 4, z: 8, core: 2. Of those that a mesh axis runs over, the one named last changes fastest.
Arguments:
- block_input: bfloat16 [8, 256, 5120], P(None, 'seq'), may hold values from -6 to 6
- accepted: bfloat16 [8, 256, 5120], P(None, 'seq'), may hold values from -6 to 6
- accept_mask: int32 [8, 256], P(None, 'seq'), may hold values 0 or 1
- cache_lengths: int32 [8], replicated, may hold values from 1 to 8192, as said below
- page_table: int32 [512], replicated, may hold values from 0 to 511, each once
- norm_gain: float32 [5120], replicated, may hold values from 0.1 to 1.9
- w_query: bfloat16 [5120, 3072], P('seq', 'head'), may hold values from -0.078125 to 0.078125
- w_key: bfloat16 [5120, 3072], P('seq', 'head'), may hold values from -0.078125 to 0.078125
- w_value: bfloat16 [5120, 3072], P('seq', 'head'), may hold values from -0.25 to 0.25
- w_out: bfloat16 [5120, 3072], P('seq', 'head'), may hold values from -0.109375 to 0.109375
- key_cache: bfloat16 [512, 128, 3072], P('seq', None, 'head')
- value_cache: bfloat16 [512, 128, 3072], P('seq', None, 'head'), may hold values from -18 to 18
Outputs:
- first_out: bfloat16 [8, 256, 5120], P(None, 'seq', 'head')
- second_out: bfloat16 [8, 256, 5120], P(None, 'seq', 'head')
Inputs may be any that keep to these rules, and one draw needn't show every extreme that they name: `cache_lengths`: max(1, 4) requests, chosen at random, hold (63) * 128 + 1 to 8192 cached tokens, one of them exactly 8192; the others hold 1 to 256. `page_table`: A permutation of the 512 pool pages; entry r * 64 + j is the pool page of cached positions j * 128 to (j + 1) * 128 - 1 of request r.
All inputs are finite; a program needn't handle non-finite values. No bound on the sum of `accept_mask` on one device may be relied on, other than what follows from the above.
Results may differ from a plain program's by a relative error of at most 0.024.
The roundings to bfloat16 on the way count: a program that leaves them out, or rounds other values in their place, can miss the bound.
Values may be sent and summed in bfloat16 or wider, within the bound.
A program may use at most 128 MiB of HBM per device.

v0:
```python
import jax
import jax.numpy as jnp
from jax import lax
from jax.sharding import PartitionSpec as P

HD = 128
PAGE = 128
MAXP = 64
masked_score = -1e30


def rotate(vectors, positions):
    half_width = vectors.shape[-1] // 2
    frequency = 10000.0 ** (-(jnp.arange(half_width).astype(jnp.float32) * 2.0) / vectors.shape[-1])
    angles = positions[..., None, None] * frequency
    cosine = jnp.cos(angles)
    sine_part = jnp.sin(angles)
    front_half = vectors[..., :half_width]
    back_half = vectors[..., half_width:]
    return jnp.concatenate(
        [front_half * cosine - back_half * sine_part, back_half * cosine + front_half * sine_part],
        axis=-1,
    )


def normalize(inputs, norm_gain):
    widened = inputs.astype(jnp.float32)
    inverse = lax.rsqrt(jnp.mean(widened * widened, axis=-1, keepdims=True) + 1e-05)
    return (widened * inverse * norm_gain).astype(jnp.bfloat16)


def per_device(
    block_input,
    accepted,
    accept_mask,
    cache_lengths,
    page_table,
    norm_gain,
    w_query,
    w_key,
    w_value,
    w_out,
    key_cache,
    value_cache,
):
    seq_place = lax.axis_index("seq")
    requests, part_len, model_width = block_input.shape
    local_width = w_query.shape[1]
    local_heads = local_width // HD
    row_count = 2 * requests * part_len
    swapped = jnp.where(accept_mask[:, :, None] == 1, accepted, block_input)
    token_rows = normalize(jnp.stack([block_input, swapped]), norm_gain).reshape(
        row_count, model_width
    )
    full_query, full_key, full_value, out_weight = (
        lax.all_gather(w_query, "seq", axis=0, tiled=True),
        lax.all_gather(w_key, "seq", axis=0, tiled=True),
        lax.all_gather(w_value, "seq", axis=0, tiled=True),
        lax.all_gather(w_out, "seq", axis=0, tiled=True),
    )
    query_rows = jnp.dot(token_rows, full_query, preferred_element_type=jnp.float32)
    key_rows = jnp.dot(token_rows, full_key, preferred_element_type=jnp.float32)
    value_rows = jnp.dot(token_rows, full_value, preferred_element_type=jnp.float32)
    positions = (
        cache_lengths[:, None]
        + seq_place * part_len
        + jnp.arange(part_len, dtype=jnp.int32)[None, :]
    ).astype(jnp.float32)
    shaped = (2, requests, part_len, local_heads, HD)
    new_queries = rotate(query_rows.reshape(shaped), positions).astype(jnp.bfloat16)
    new_keys = rotate(key_rows.reshape(shaped), positions).astype(jnp.bfloat16)
    new_values = value_rows.reshape(shaped).astype(jnp.bfloat16)
    every_query = lax.all_gather(new_queries, "seq", axis=2, tiled=True)
    pages_here = key_cache.shape[0]
    page_ids = seq_place * pages_here + jnp.arange(pages_here, dtype=jnp.int32)
    table_slots = jnp.arange(page_table.shape[0], dtype=jnp.int32)
    slot_of = jnp.sum(
        jnp.where(page_table[None, :] == page_ids[:, None], table_slots[None, :], 0), axis=1
    )
    page_owner = slot_of // MAXP
    owner_match = page_owner[:, None] == jnp.arange(requests, dtype=jnp.int32)[None, :]
    owner_length = jnp.sum(jnp.where(owner_match, cache_lengths[None, :], 0), axis=1)
    offsets = (slot_of % MAXP)[:, None] * PAGE + jnp.arange(PAGE, dtype=jnp.int32)[None, :]
    live_mask = (offsets < owner_length[:, None])[:, None, None, :]
    owner_hot = owner_match.astype(jnp.float32)
    cached_keys = key_cache.reshape(pages_here, PAGE, local_heads, HD)
    cached_values = value_cache.reshape(pages_here, PAGE, local_heads, HD)
    score_scale = HD ** (-0.5)

    def local_part(pass_items):
        pass_queries, pass_keys, pass_values = pass_items
        page_queries = jnp.take(pass_queries, page_owner, axis=0)
        scores = (
            jnp.einsum(
                "pqhd,pkhd->pqhk", page_queries, cached_keys, preferred_element_type=jnp.float32
            )
            * score_scale
        )
        scores = jnp.where(live_mask, scores, masked_score)
        page_peak = jnp.max(scores, axis=-1)
        weights = jnp.where(live_mask, jnp.exp(scores - page_peak[..., None]), 0.0)
        page_total = jnp.sum(weights, axis=-1)
        page_out = jnp.einsum(
            "pqhk,pkhd->pqhd",
            weights.astype(jnp.bfloat16),
            cached_values,
            preferred_element_type=jnp.float32,
        )
        owner_peak = jnp.max(
            jnp.where(owner_match[:, :, None, None], page_peak[:, None], masked_score), axis=0
        )
        factor = jnp.exp(page_peak - jnp.take(owner_peak, page_owner, axis=0))
        cache_total = jnp.einsum(
            "pr,pqh->rqh", owner_hot, page_total * factor, precision=lax.Precision.HIGHEST
        )
        cache_out = jnp.einsum(
            "pr,pqhd->rqhd",
            owner_hot,
            page_out * factor[..., None],
            precision=lax.Precision.HIGHEST,
        )
        block_scores = (
            jnp.einsum(
                "rqhd,rkhd->rqhk", pass_queries, pass_keys, preferred_element_type=jnp.float32
            )
            * score_scale
        )
        block_peak = jnp.max(block_scores, axis=-1)
        block_weights = jnp.exp(block_scores - block_peak[..., None])
        block_total = jnp.sum(block_weights, axis=-1)
        block_out = jnp.einsum(
            "rqhk,rkhd->rqhd",
            block_weights,
            pass_values.astype(jnp.float32),
            precision=lax.Precision.HIGHEST,
        )
        row_peak = jnp.maximum(owner_peak, block_peak)
        cache_factor = jnp.exp(owner_peak - row_peak)
        block_factor = jnp.exp(block_peak - row_peak)
        joined_total = cache_total * cache_factor + block_total * block_factor
        joined_out = cache_out * cache_factor[..., None] + block_out * block_factor[..., None]
        return (row_peak, joined_total, joined_out)

    row_peak, row_total, row_out = lax.map(local_part, (every_query, new_keys, new_values))
    overall = lax.pmax(row_peak, "seq")
    rescale = jnp.exp(row_peak - overall)
    summed_out, summed_total = (
        lax.psum_scatter(row_out * rescale[..., None], "seq", scatter_dimension=2, tiled=True),
        lax.psum_scatter(row_total * rescale, "seq", scatter_dimension=2, tiled=True),
    )
    context = (
        (summed_out / summed_total[..., None]).astype(jnp.bfloat16).reshape(row_count, local_width)
    )
    partial_value = lax.dot_general(
        context, out_weight, (((1,), (1,)), ((), ())), preferred_element_type=jnp.float32
    )
    own_share = lax.psum_scatter(partial_value, "head", scatter_dimension=1, tiled=True).astype(
        jnp.bfloat16
    )
    result = own_share.reshape(2, requests, part_len, own_share.shape[1])
    return (result[0], result[1])


def solution(mesh):
    placed = (
        P(None, "seq", None),
        P(None, "seq", None),
        P(None, "seq"),
        P(),
        P(),
        P(),
        P("seq", "head"),
        P("seq", "head"),
        P("seq", "head"),
        P("seq", "head"),
        P("seq", None, "head"),
        P("seq", None, "head"),
    )
    return jax.shard_map(
        per_device,
        mesh=mesh,
        in_specs=placed,
        out_specs=(P(None, "seq", "head"), P(None, "seq", "head")),
        check_vma=False,
    )
```

profile of v0, /device:TPU:2, one launch (start us, length us, event | category | flops | bytes accessed | tf_op | source)
XLA Modules:
  0.0 919.2 jit_solution(8133665721481068145)
XLA Ops:
  10.1 1.4 select_bitcast_fusion
  11.6 1.4 fusion.53
  13.3 80.1 %all-gather.10.cloned.1.call-done = bf16[5120,384]{1,0:T(8,128)(2,1)} async-done(((bf16[160,384]{1,0:T(8,128)(2,1)}), bf16[5120,384]{1,0:T(8,128)(2,1)}) %all-gather.10.cloned.1.call-update) | async-done | bytes 3932176 | tf_op jit(solution)/shard_map/all_gather | solution.py:57
  93.4 6.3 copy.77
  99.7 74.6 %all-gather.6.cloned.1.call-done = bf16[5120,384]{1,0:T(8,128)(2,1)} async-done(((bf16[160,384]{1,0:T(8,128)(2,1)}), bf16[5120,384]{1,0:T(8,128)(2,1)}) %all-gather.6.cloned.1.call-update) | async-done | bytes 3932176 | tf_op jit(solution)/shard_map/all_gather | solution.py:56
  174.3 6.3 copy.75
  180.6 3.5 fusion.59
  184.2 1.3 fusion.61
  186.5 1.9 copy.76
  188.4 1.6 copy.80
  190.0 1.9 copy.78
  192.0 1.6 copy.81
  193.9 61.3 %all-gather.12.cloned.1.call-done = bf16[5120,384]{1,0:T(8,128)(2,1)} async-done(((bf16[160,384]{1,0:T(8,128)(2,1)}), bf16[5120,384]{1,0:T(8,128)(2,1)}) %all-gather.12.cloned.1.call-update) | async-done | bytes 3932176 | tf_op jit(solution)/shard_map/all_gather | solution.py:58
  255.2 6.3 copy.79
  262.2 4.0 convolution_convert_fusion
  266.2 69.3 %all-gather.8.cloned.1.call-done = bf16[2,8,256,3,128]{4,2,3,1,0:T(8,128)(2,1)} async-done(((bf16[2,8,8,3,128]{4,2,3,1,0:T(8,128)(2,1)}), bf16[2,8,256,3,128]{4,2,3,1,0:T(8,128)(2,1)}) %all-gather.8.cloned.1.call-update) | async-done | bytes 3145744 | tf_op jit(solution)/shard_map/all_gather | solution.py:73
  335.5 82.3 %while.16 = (s32[]{:T(128)}, f32[2,8,256,3]{2,1,3,0:T(8,128)}, f32[2,8,256,3]{2,1,3,0:T(8,128)}, f32[2,8,256,3,128]{4,2,3,1,0:T(8,128)}, s32[16]{0:T(128)S(1)}, ...) while((s32[]{:T(128)}, f32[2,8,256,3]{2,1,3,0:T(8,128)}, ...), condition=%wide.region_9.10_spmd.clone.clone, body=%wide.region_3.9_spmd.clone.clone.sunk | while | flops 1071998720 | bytes 124305208 | solution.py:144
  335.5 1.5 dynamic-slice_bitcast_fusion.3
  337.0 2.7 gather_fusion
  339.8 3.0 bitcast_reduce_fusion.2
  342.8 2.2 fusion.98
  346.8 8.2 bitcast_multiply_fusion.4
  355.6 1.0 copy.127
  356.6 1.0 copy.128
  357.7 2.2 fusion.102
  359.9 2.3 copy.126
  362.2 11.2 %fusion.103 = f32[1,8,256,3,128]{4,1,3,2,0:T(8,128)S(1)} fusion(f32[8,3,128,256]{2,0,1,3:T(8,128)} %copy.126, f32[16,256,3,128]{3,1,2,0:T(8,128)} %bitcast_multiply_fusion.4, f32[8,256,3]{0,2,1:T(4,128)} %copy.127, f32[8,256,3]{0,2,1:T(4,128)} %copy.128, s32[16]{0:T(128)S(1)} %get-tuple-element.340), kind=kOutput, calls=%fused_computation.19.clone.1 | convolution fusion | flops 153354496 | bytes 12632128 | tf_op jit(solution)/shard_map/while/body/eval_jaxpr/pr,pqhd->rqhd/dot_general | solution.py:116
  373.5 2.2 copy_dynamic-update-slice_fusion.2
  376.6 1.5 dynamic-slice_bitcast_fusion.3
  378.2 2.7 gather_fusion
  380.9 3.0 bitcast_reduce_fusion.2
  383.9 2.2 fusion.98
  387.9 8.2 bitcast_multiply_fusion.4
  396.7 1.0 copy.127
  397.8 1.0 copy.128
  398.8 2.2 fusion.102
  401.0 2.3 copy.126
  403.4 11.2 %fusion.103 = f32[1,8,256,3,128]{4,1,3,2,0:T(8,128)S(1)} fusion(f32[8,3,128,256]{2,0,1,3:T(8,128)} %copy.126, f32[16,256,3,128]{3,1,2,0:T(8,128)} %bitcast_multiply_fusion.4, f32[8,256,3]{0,2,1:T(4,128)} %copy.127, f32[8,256,3]{0,2,1:T(4,128)} %copy.128, s32[16]{0:T(128)S(1)} %get-tuple-element.340), kind=kOutput, calls=%fused_computation.19.clone.1 | convolution fusion | flops 153354496 | bytes 12632128 | tf_op jit(solution)/shard_map/while/body/eval_jaxpr/pr,pqhd->rqhd/dot_general | solution.py:116
  414.6 2.3 copy_dynamic-update-slice_fusion.2
  417.8 137.8 %pmax.7 = f32[2,8,256,3]{2,1,3,0:T(8,128)S(1)} all-reduce(f32[2,8,256,3]{2,1,3,0:T(8,128)} %get-tuple-element.72), channel_id=1, replica_groups=mesh['seq'=32,'head'=8] {'seq'}, use_global_device_ids=true, to_apply=%region_10.11 | all-reduce | flops 12288 | bytes 98304 | tf_op jit(solution)/shard_map/pmax | solution.py:145
  556.5 7.3 broadcast_multiply_fusion
  565.7 140.1 %all-reduce = f32[2,8,256,3]{2,1,3,0:T(8,128)S(1)} all-reduce(f32[2,8,256,3]{2,1,3,0:T(8,128)S(1)} %get-tuple-element.201), channel_id=3, replica_groups=mesh['seq'=32,'head'=8] {'seq'}, use_global_device_ids=true, to_apply=%region_12.13.clone | all-reduce | flops 12288 | bytes 98304
  706.0 82.0 %reduce-scatter.4.cloned.1.call-done = f32[2,8,8,3,128]{4,2,3,1,0:T(8,128)} async-done(((f32[2,8,256,3,128]{4,2,3,1,0:T(8,128)}), f32[2,8,8,3,128]{4,2,3,1,0:T(8,128)}) %reduce-scatter.4.cloned.1.call-update) | async-done | bytes 196624 | tf_op jit(solution)/shard_map/reduce_scatter | solution.py:148
  788.0 1.0 divide_convert_fusion
  789.1 80.8 %all-gather.14.cloned.1.call-done = bf16[5120,384]{1,0:T(8,128)(2,1)} async-done(((bf16[160,384]{1,0:T(8,128)(2,1)}), bf16[5120,384]{1,0:T(8,128)(2,1)}) %all-gather.14.cloned.1.call-update) | async-done | bytes 3932176 | tf_op jit(solution)/shard_map/all_gather | solution.py:59
  869.8 5.0 fusion.66
  874.8 35.8 %reduce-scatter.6.cloned.1.call-done = f32[128,640]{1,0:T(8,128)} async-done(((f32[128,5120]{1,0:T(8,128)}), f32[128,640]{1,0:T(8,128)}) %reduce-scatter.6.cloned.1.call-update) | async-done | bytes 327696 | tf_op jit(solution)/shard_map/reduce_scatter | solution.py:157
  910.7 1.0 convert_element_type.66
  (112 shorter events, 14.7 us)
Async XLA Ops:
  7.2 5.8 copy-start.13
  7.2 86.2 %all-gather.10.cloned.1.call-start = ((), (), s32[]{:S(2)}) async-start(), calls=%async_computation.4 | async-start | bytes 4055040 | tf_op jit(solution)/shard_map/all_gather | solution.py:57
  7.9 166.4 %all-gather.6.cloned.1.call-start = ((), (), s32[]{:S(2)}) async-start(), calls=%async_computation.2 | async-start | bytes 4055040 | tf_op jit(solution)/shard_map/all_gather | solution.py:56
  8.7 246.5 %all-gather.12.cloned.1.call-start = ((), (), s32[]{:S(2)}) async-start(), calls=%async_computation.5 | async-start | bytes 4055040 | tf_op jit(solution)/shard_map/all_gather | solution.py:58
  9.4 326.1 %all-gather.8.cloned.1.call-start = ((), (), s32[]{:S(2)}) async-start(), calls=%async_computation.3 | async-start | bytes 3244032 | tf_op jit(solution)/shard_map/all_gather | solution.py:73
  174.3 6.3 copy-start.3
  174.3 6.3 copy-start.12
  180.6 3.5 copy-start.2
  186.4 601.6 %reduce-scatter.4.cloned.1.call-start = ((), (), s32[]{:S(2)}) async-start(), calls=%async_computation.6 | async-start | bytes 6488064 | tf_op jit(solution)/shard_map/reduce_scatter | solution.py:148
  190.0 3.6 copy-start.11
  337.0 2.8 copy-start.4
  342.8 2.6 copy-start
  345.4 1.4 copy-start.5
  346.8 8.2 copy-start.1
  346.8 8.2 copy-start.6
  373.4 2.3 copy-start.9
  373.4 2.5 copy-start.7
  375.9 0.6 copy-start.10
  376.0 0.6 copy-start.8
  378.2 2.8 copy-start.4
  383.9 2.6 copy-start
  386.5 1.4 copy-start.5
  387.9 8.3 copy-start.1
  387.9 8.3 copy-start.6
  414.6 2.4 copy-start.9
  414.6 2.6 copy-start.7
  417.1 0.6 copy-start.10
  417.2 0.6 copy-start.8
  563.8 0.7 copy-start.14
  563.9 306.0 %all-gather.14.cloned.1.call-start = ((), (), s32[]{:S(2)}) async-start(), calls=%async_computation.7 | async-start | bytes 4055040 | tf_op jit(solution)/shard_map/all_gather | solution.py:59
  564.4 346.2 %reduce-scatter.6.cloned.1.call-start = ((), (), s32[]{:S(2)}) async-start(), calls=%async_computation.8 | async-start | bytes 2949120 | tf_op jit(solution)/shard_map/reduce_scatter | solution.py:157
Sparse Core Ops, SparseCore 0:
  10.6 82.7 all-gather.9
  96.0 78.2 all-gather.5
  176.9 78.2 all-gather.11
  257.5 77.9 all-gather.7
  564.0 223.9 reduce-scatter.3
  790.8 79.0 all-gather.13
  874.9 35.6 reduce-scatter.5
where the time goes:
time: 920 us; the launch traced here: 919 us
  waiting for transfers between devices  487 us (53%)
  blocking collectives  278 us (30%)
  matrix products  64.6 us (7%)
  local copies, waits for them, and re-layouts  53.1 us (6%)
  other arithmetic  21.4 us (2%)
  between operations  14.9 us (2%)
    unnamed x1, blocking collectives  140 us
    pmax x1, blocking collectives, per_device(): overall = lax.pmax(row_peak, 'seq')  138 us
    reduce_scatter x1, waiting for transfers between devices, per_device(): lax.psum_scatter(row_out * rescale[..., None], 'seq', scatter_dimension=2...  82 us
    all_gather x1, waiting for transfers between devices, per_device(): lax.all_gather(w_out, 'seq', axis=0, tiled=True)  80.8 us
    all_gather x1, waiting for transfers between devices, per_device(): lax.all_gather(w_key, 'seq', axis=0, tiled=True)  80.1 us
    all_gather x1, waiting for transfers between devices, per_device(): lax.all_gather(w_query, 'seq', axis=0, tiled=True)  74.6 us
    all_gather x1, waiting for transfers between devices, per_device(): every_query = lax.all_gather(new_queries, 'seq', axis=2, tiled=True)  69.3 us
    all_gather x1, waiting for transfers between devices, per_device(): lax.all_gather(w_value, 'seq', axis=0, tiled=True)  61.3 us
  transfers between devices with their start and end apart: 7, of which 7 were waited for; matrix products, arithmetic and copies ran while one was open for 5% of the time, Pallas kernels for 0%

commit v1 on v0

--- a/solution.py
+++ b/solution.py
@@ -70,7 +70,9 @@
     new_queries = rotate(query_rows.reshape(shaped), positions).astype(jnp.bfloat16)
     new_keys = rotate(key_rows.reshape(shaped), positions).astype(jnp.bfloat16)
     new_values = value_rows.reshape(shaped).astype(jnp.bfloat16)
-    every_query = lax.all_gather(new_queries, "seq", axis=2, tiled=True)
+    every_query = jnp.concatenate(
+        lax.all_to_all(jnp.stack([new_queries] * lax.axis_size("seq")), "seq", 0, 0), axis=2
+    )
     pages_here = key_cache.shape[0]
     page_ids = seq_place * pages_here + jnp.arange(pages_here, dtype=jnp.int32)
     table_slots = jnp.arange(page_table.shape[0], dtype=jnp.int32)

time: 920 us -> 886 us (0.963)
  waiting for transfers between devices: 487 us -> 437 us
    all_gather x1 -> x0, waiting for transfers between devices: 69.3 us -> none  [per_device(): every_query = lax.all_gather(new_queries, 'seq', axis=2, tiled=True)]
    all_gather x1, waiting for transfers between devices: 61.3 us -> 79.8 us  [per_device(): lax.all_gather(w_value, 'seq', axis=0, tiled=True)]
  transfers between devices with their start and end apart: 7 -> 7, of which waited for: 7 -> 6; matrix products, arithmetic and copies ran while one was open for 5% -> 5% of each run, Pallas kernels for 0% -> 0%
where the time goes in v1:
time: 886 us; the launch traced here: 885 us
  waiting for transfers between devices  437 us (49%)
  blocking collectives  277 us (31%)
  matrix products  65 us (7%)
  local copies, waits for them, and re-layouts  61.4 us (7%)
  other arithmetic  21 us (2%)
  between operations  14.9 us (2%)
    unnamed x1, blocking collectives  140 us
    pmax x1, blocking collectives, per_device(): overall = lax.pmax(row_peak, 'seq')  137 us
    reduce_scatter x1, waiting for transfers between devices, per_device(): lax.psum_scatter(row_out * rescale[..., None], 'seq', scatter_dimension=2...  83.6 us
    all_gather x1, waiting for transfers between devices, per_device(): lax.all_gather(w_out, 'seq', axis=0, tiled=True)  80.7 us
    all_gather x1, waiting for transfers between devices, per_device(): lax.all_gather(w_key, 'seq', axis=0, tiled=True)  79.9 us
    all_gather x1, waiting for transfers between devices, per_device(): lax.all_gather(w_value, 'seq', axis=0, tiled=True)  79.8 us
    all_gather x1, waiting for transfers between devices, per_device(): lax.all_gather(w_query, 'seq', axis=0, tiled=True)  74.6 us
    reduce_scatter x1, waiting for transfers between devices, per_device(): lax.psum_scatter(partial_value, 'head', scatter_dimension=1, tiled=True)  35.9 us
  transfers between devices with their start and end apart: 7, of which 6 were waited for; matrix products, arithmetic and copies ran while one was open for 5% of the time, Pallas kernels for 0%

profile of v1, /device:TPU:2, one launch (start us, length us, event | category | flops | bytes accessed | tf_op | source)
XLA Modules:
  0.0 884.6 jit_solution(8730756467640048298)
XLA Ops:
  10.1 1.4 select_bitcast_fusion
  11.5 1.7 fusion.53
  13.5 79.9 %all-gather.7.cloned.1.call-done = bf16[5120,384]{1,0:T(8,128)(2,1)} async-done(((bf16[160,384]{1,0:T(8,128)(2,1)}), bf16[5120,384]{1,0:T(8,128)(2,1)}) %all-gather.7.cloned.1.call-update) | async-done | bytes 3932176 | tf_op jit(solution)/shard_map/all_gather | solution.py:57
  93.4 6.3 copy.100
  99.7 74.6 %all-gather.5.cloned.1.call-done = bf16[5120,384]{1,0:T(8,128)(2,1)} async-done(((bf16[160,384]{1,0:T(8,128)(2,1)}), bf16[5120,384]{1,0:T(8,128)(2,1)}) %all-gather.5.cloned.1.call-update) | async-done | bytes 3932176 | tf_op jit(solution)/shard_map/all_gather | solution.py:56
  174.3 6.3 copy.97
  180.6 3.5 fusion.59
  184.2 1.3 fusion.61
  185.8 2.4 stack.11
  188.1 7.3 all-to-all-start
  195.5 2.6 copy.99
  198.1 2.6 copy.103
  200.7 2.6 copy.101
  203.3 2.6 copy.104
  206.2 79.8 %all-gather.9.cloned.1.call-done = bf16[5120,384]{1,0:T(8,128)(2,1)} async-done(((bf16[160,384]{1,0:T(8,128)(2,1)}), bf16[5120,384]{1,0:T(8,128)(2,1)}) %all-gather.9.cloned.1.call-update) | async-done | bytes 3932176 | tf_op jit(solution)/shard_map/all_gather | solution.py:58
  286.0 6.3 copy.102
  293.0 4.4 convolution_convert_fusion
  297.5 2.6 copy.133
  300.0 82.3 %while.16 = (s32[]{:T(128)}, f32[2,8,256,3]{2,1,3,0:T(8,128)}, f32[2,8,256,3]{2,1,3,0:T(8,128)}, f32[2,8,256,3,128]{4,2,3,1,0:T(8,128)}, s32[16]{0:T(128)S(1)}, ...) while((s32[]{:T(128)}, f32[2,8,256,3]{2,1,3,0:T(8,128)}, ...), condition=%wide.region_9.10_spmd.clone.clone, body=%wide.region_3.9_spmd.clone.clone.sunk | while | flops 1071998720 | bytes 124305208 | solution.py:146
  300.0 1.5 dynamic-slice_bitcast_fusion.3
  301.6 2.7 gather_fusion
  304.3 3.0 bitcast_reduce_fusion.2
  307.3 2.2 fusion.98
  311.3 8.2 bitcast_multiply_fusion.4
  320.1 1.0 copy.152
  321.2 1.0 copy.153
  322.2 2.2 fusion.102
  324.4 2.3 copy.151
  326.8 11.2 %fusion.103 = f32[1,8,256,3,128]{4,1,3,2,0:T(8,128)S(1)} fusion(f32[8,3,128,256]{2,0,1,3:T(8,128)} %copy.151, f32[16,256,3,128]{3,1,2,0:T(8,128)} %bitcast_multiply_fusion.4, f32[8,256,3]{0,2,1:T(4,128)} %copy.152, f32[8,256,3]{0,2,1:T(4,128)} %copy.153, s32[16]{0:T(128)S(1)} %get-tuple-element.352), kind=kOutput, calls=%fused_computation.19.clone.1 | convolution fusion | flops 153354496 | bytes 12632128 | tf_op jit(solution)/shard_map/while/body/eval_jaxpr/pr,pqhd->rqhd/dot_general | solution.py:118
  338.0 2.2 copy_dynamic-update-slice_fusion.2
  341.1 1.5 dynamic-slice_bitcast_fusion.3
  342.7 2.7 gather_fusion
  345.4 3.0 bitcast_reduce_fusion.2
  348.5 2.2 fusion.98
  352.4 8.2 bitcast_multiply_fusion.4
  361.3 1.0 copy.152
  363.3 2.2 fusion.102
  365.5 2.3 copy.151
  367.9 11.2 %fusion.103 = f32[1,8,256,3,128]{4,1,3,2,0:T(8,128)S(1)} fusion(f32[8,3,128,256]{2,0,1,3:T(8,128)} %copy.151, f32[16,256,3,128]{3,1,2,0:T(8,128)} %bitcast_multiply_fusion.4, f32[8,256,3]{0,2,1:T(4,128)} %copy.152, f32[8,256,3]{0,2,1:T(4,128)} %copy.153, s32[16]{0:T(128)S(1)} %get-tuple-element.352), kind=kOutput, calls=%fused_computation.19.clone.1 | convolution fusion | flops 153354496 | bytes 12632128 | tf_op jit(solution)/shard_map/while/body/eval_jaxpr/pr,pqhd->rqhd/dot_general | solution.py:118
  379.1 2.3 copy_dynamic-update-slice_fusion.2
  382.3 136.9 %pmax.7 = f32[2,8,256,3]{2,1,3,0:T(8,128)S(1)} all-reduce(f32[2,8,256,3]{2,1,3,0:T(8,128)} %get-tuple-element.72), channel_id=1, replica_groups=mesh['seq'=32,'head'=8] {'seq'}, use_global_device_ids=true, to_apply=%region_10.11 | all-reduce | flops 12288 | bytes 98304 | tf_op jit(solution)/shard_map/pmax | solution.py:147
  520.1 7.3 broadcast_multiply_fusion
  529.3 140.4 %all-reduce = f32[2,8,256,3]{2,1,3,0:T(8,128)S(1)} all-reduce(f32[2,8,256,3]{2,1,3,0:T(8,128)S(1)} %get-tuple-element.213), channel_id=3, replica_groups=mesh['seq'=32,'head'=8] {'seq'}, use_global_device_ids=true, to_apply=%region_12.13.clone | all-reduce | flops 12288 | bytes 98304
  669.8 83.6 %reduce-scatter.4.cloned.1.call-done = f32[2,8,8,3,128]{4,2,3,1,0:T(8,128)} async-done(((f32[2,8,256,3,128]{4,2,3,1,0:T(8,128)}), f32[2,8,8,3,128]{4,2,3,1,0:T(8,128)}) %reduce-scatter.4.cloned.1.call-update) | async-done | bytes 196624 | tf_op jit(solution)/shard_map/reduce_scatter | solution.py:150
  753.5 1.0 divide_convert_fusion
  754.5 80.7 %all-gather.11.cloned.1.call-done = bf16[5120,384]{1,0:T(8,128)(2,1)} async-done(((bf16[160,384]{1,0:T(8,128)(2,1)}), bf16[5120,384]{1,0:T(8,128)(2,1)}) %all-gather.11.cloned.1.call-update) | async-done | bytes 3932176 | tf_op jit(solution)/shard_map/all_gather | solution.py:59
  835.2 5.0 fusion.66
  840.2 35.9 %reduce-scatter.6.cloned.1.call-done = f32[128,640]{1,0:T(8,128)} async-done(((f32[128,5120]{1,0:T(8,128)}), f32[128,640]{1,0:T(8,128)}) %reduce-scatter.6.cloned.1.call-update) | async-done | bytes 327696 | tf_op jit(solution)/shard_map/reduce_scatter | solution.py:159
  (115 shorter events, 16.0 us)
Async XLA Ops:
  7.2 6.0 copy-start.14
  7.2 86.2 %all-gather.7.cloned.1.call-start = ((), (), s32[]{:S(2)}) async-start(), calls=%async_computation.4 | async-start | bytes 4055040 | tf_op jit(solution)/shard_map/all_gather | solution.py:57
  7.9 166.4 %all-gather.5.cloned.1.call-start = ((), (), s32[]{:S(2)}) async-start(), calls=%async_computation.3 | async-start | bytes 4055040 | tf_op jit(solution)/shard_map/all_gather | solution.py:56
  8.7 277.4 %all-gather.9.cloned.1.call-start = ((), (), s32[]{:S(2)}) async-start(), calls=%async_computation.5 | async-start | bytes 4055040 | tf_op jit(solution)/shard_map/all_gather | solution.py:58
  11.5 172.6 %copy-start.4 = (bf16[1,8,8,5120]{3,2,1,0:T(8,128)(2,1)}, bf16[1,8,8,5120]{3,2,1,0:T(8,128)(2,1)S(1)}, u32[]{:S(2)}) copy-start(bf16[1,8,8,5120]{3,2,1,0:T(8,128)(2,1)S(1)} %select_bitcast_fusion) | copy-start | bytes 1966084
  174.3 6.3 copy-start.3
  174.3 6.3 copy-start.13
  180.6 3.6 copy-start.2
  188.1 109.3 %all-to-all-start = ((bf16[32,2,8,8,3,128]{5,3,4,2,1,0:T(8,128)(2,1)}), bf16[32,2,8,8,3,128]{5,3,4,2,1,0:T(8,128)(2,1)S(1)}, u32[]{:S(2)}, u32[]{:S(2)}) async-start(bf16[32,2,8,8,3,128]{5,3,4,2,1,0:T(8,128)(2,1)} %stack.11), calls=%async_computation | async-start | bytes 6291456 | tf_op jit(solution)/shard_map/all_to_all | solution.py:74
  195.4 558.0 %reduce-scatter.4.cloned.1.call-start = ((), (), s32[]{:S(2)}) async-start(), calls=%async_computation.6 | async-start | bytes 6488064 | tf_op jit(solution)/shard_map/reduce_scatter | solution.py:150
  200.7 5.2 copy-start.12
  301.6 2.8 copy-start.5
  307.3 2.6 copy-start
  309.9 1.4 copy-start.6
  311.3 8.3 copy-start.1
  311.3 8.3 copy-start.7
  338.0 2.3 copy-start.10
  338.0 2.5 copy-start.8
  340.5 0.6 copy-start.11
  340.5 0.6 copy-start.9
  342.7 2.8 copy-start.5
  348.4 2.6 copy-start
  351.0 1.4 copy-start.6
  352.4 8.2 copy-start.1
  352.4 8.2 copy-start.7
  379.1 2.4 copy-start.10
  379.1 2.6 copy-start.8
  381.6 0.6 copy-start.11
  381.7 0.6 copy-start.9
  527.4 0.7 copy-start.15
  527.4 307.8 %all-gather.11.cloned.1.call-start = ((), (), s32[]{:S(2)}) async-start(), calls=%async_computation.7 | async-start | bytes 4055040 | tf_op jit(solution)/shard_map/all_gather | solution.py:59
  528.0 348.1 %reduce-scatter.6.cloned.1.call-start = ((), (), s32[]{:S(2)}) async-start(), calls=%async_computation.8 | async-start | bytes 2949120 | tf_op jit(solution)/shard_map/reduce_scatter | solution.py:159
Sparse Core Ops, SparseCore 0:
  10.6 82.7 all-gather.6
  96.0 78.2 all-gather.4
  176.9 109.1 all-gather.8
  527.5 225.8 reduce-scatter.3
  756.2 78.9 all-gather.10
  840.3 35.7 reduce-scatter.5
